TPU v7x, 256 devices: a whole 4x4x8 slice. The times are simulated.
256 devices in a mesh: seq: 64 (over x, z, core), head: 4 (over y).
Axes of the slice: x: 4, y: 4, z: 8, core: 2. Of those that a mesh axis runs over, the one named last changes fastest.
Arguments:
- queries: bfloat16 [32768, 4096], P('seq', 'head'), may hold values from -6 to 6
- key_input: bfloat16 [32768, 4096], P('seq', 'head'), may hold values from -6 to 6
- value_input: bfloat16 [32768, 4096], P('seq', 'head'), may hold values from -40 to 40
- gate_input: bfloat16 [32768, 4096], P('seq', 'head'), may hold values from -8 to 8
- kv_state: float32 [32, 128, 128], P('head'), may hold values from -512 to 512
- norm_gain: float32 [4096], replicated, may hold values from 0.25 to 1.75
- out_weight: bfloat16 [4096, 4096], P('head', 'seq'), may hold values from -0.09375 to 0.09375
Outputs:
- output: bfloat16 [32768, 4096], P(('seq', 'head'))
All inputs are finite; a program needn't handle non-finite values.
Results may differ from a plain program's by a relative error of at most 0.02.
Values may be sent and summed in bfloat16 or wider, within the bound.
A program may use at most 128 MiB of HBM per device.

v0:
```python
import jax
import jax.numpy as jnp
from jax import lax
from jax.sharding import PartitionSpec as P

DH = 128
BLOCK = 512
epsilon = 1e-05


def entering(value, axis, join, neutral):
    place = lax.axis_index(axis)
    gathered = lax.all_gather(value.astype(jnp.bfloat16), axis)
    state = jnp.zeros_like(value) + jnp.asarray(neutral, value.dtype)

    def one(turn, state):
        return join(state, lax.dynamic_index_in_dim(gathered, turn, 0, False).astype(value.dtype))

    return lax.fori_loop(0, place, one, state)


def add_states(earlier, later):
    return earlier + later


def gated_norm(attn_rows, gate_rows, gain_part, total_width, square_sum):
    attn_float = attn_rows.astype(jnp.float32)
    scale = lax.rsqrt(square_sum / total_width + epsilon)
    normed = attn_float * scale[:, None] * gain_part[None, :]
    return (normed * jax.nn.sigmoid(gate_rows.astype(jnp.float32))).astype(jnp.bfloat16)


def shards(queries, key_input, value_input, gate_input, kv_state, norm_gain, out_weight):
    tok_rows = queries.shape[0]
    local_width = queries.shape[1]
    local_heads = local_width // DH
    num_blocks = tok_rows // BLOCK
    block_shape = (num_blocks, BLOCK, local_heads, DH)
    q_blocks = queries.reshape(block_shape)
    k_blocks = key_input.reshape(block_shape)
    v_blocks = value_input.reshape(block_shape)
    block_states = jnp.einsum(
        "nthd,nthe->nhde", k_blocks, v_blocks, preferred_element_type=jnp.float32
    )
    own_total = jnp.sum(block_states, axis=0)
    prefix = entering(own_total, "seq", add_states, jnp.zeros_like(own_total))
    start_state = kv_state + prefix
    running = jnp.cumsum(block_states, axis=0) - block_states
    before = start_state[None] + running
    carried_part = jnp.einsum(
        "nthd,nhde->nthe", q_blocks.astype(jnp.float32), before, precision=lax.Precision.HIGHEST
    )
    scores = jnp.einsum("nthd,nshd->nhts", q_blocks, k_blocks, preferred_element_type=jnp.float32)
    causal = jnp.arange(BLOCK)[:, None] >= jnp.arange(BLOCK)[None, :]
    weights = jnp.where(causal[None, None], scores, 0.0).astype(jnp.bfloat16)
    inner_part = jnp.einsum(
        "nhts,nshe->nthe", weights, v_blocks, preferred_element_type=jnp.float32
    )
    attn = (carried_part + inner_part).astype(jnp.bfloat16).reshape(tok_rows, local_width)
    total_width = local_width * lax.axis_size("head")
    tok_attn, tok_gate = (
        lax.all_to_all(attn, "head", split_axis=0, concat_axis=1, tiled=True),
        lax.all_to_all(gate_input, "head", split_axis=0, concat_axis=1, tiled=True),
    )
    tok_float = tok_attn.astype(jnp.float32)
    normed = gated_norm(
        tok_attn, tok_gate, norm_gain, total_width, jnp.sum(tok_float * tok_float, axis=1)
    )
    hidden = lax.all_to_all(normed, "head", split_axis=1, concat_axis=0, tiled=True)
    terms = jnp.dot(
        hidden,
        lax.all_gather(out_weight, "seq", axis=1, tiled=True),
        preferred_element_type=jnp.float32,
    )
    return lax.psum_scatter(terms.astype(jnp.bfloat16), "head", scatter_dimension=0, tiled=True)


def solution(mesh):
    in_specs = (
        P("seq", "head"),
        P("seq", "head"),
        P("seq", "head"),
        P("seq", "head"),
        P("head", None, None),
        P(),
        P("head", "seq"),
    )
    out_specs = P(("seq", "head"), None)
    return jax.shard_map(shards, mesh=mesh, in_specs=in_specs, out_specs=out_specs, check_vma=False)
```

profile of v0, /device:TPU:1, one launch (start us, length us, event | category | flops | bytes accessed | tf_op | source)
XLA Modules:
  0.0 307.6 jit_solution(3969963221888918470)
XLA Ops:
  6.5 0.0 copy-start
  6.5 0.0 all-gather.6.cloned.1.call-start
  6.5 2.9 fusion.34
  9.4 0.0 all-gather.6.cloned.1.call-update
  9.4 0.0 all-gather.4.cloned.1.call-start
  9.5 0.7 all-gather.4.cloned.1.call-update
  10.2 0.1 iota_compare_fusion
  10.3 103.8 %all-gather.6.cloned.1.call-done = bf16[512,128,128]{2,1,0:T(8,128)(2,1)} async-done(((bf16[8,128,128]{2,1,0:T(8,128)(2,1)}), bf16[512,128,128]{2,1,0:T(8,128)(2,1)}) %all-gather.6.cloned.1.call-update) | async-done | bytes 16777232 | tf_op jit(solution)/shard_map/all_gather | solution.py:13
  114.1 0.0 copy-start.2
  114.1 1.2 while.10
  114.1 1.1 convert_add_fusion.2
  115.3 0.0 copy-done
  115.3 0.0 copy-done.2
  115.3 2.4 fusion.13
  117.7 4.8 %fusion.10 = bf16[1,512,8,128]{1,3,2,0:T(8,128)(2,1)S(1)} fusion(f32[8,128,512]{2,1,0:T(8,128)} %fusion.13, pred[512,512]{1,0:T(8,128)(4,1)S(1)} %iota_compare_fusion, bf16[512,1024]{1,0:T(8,128)(2,1)S(1)} %copy-done, bf16[512,1024]{1,0:T(8,128)(2,1)} %param.11, bf16[512,1024]{1,0:T(8,128)(2,1)} %param.10), kind=kOutput, calls=%fused_computation.15 | convolution fusion | flops 1078984704 | bytes 6553600 | tf_op jit(solution)/shard_map/nhts,nshe->nthe/dot_general | solution.py:56
  122.5 0.3 all_to_all.32
  122.8 0.0 copy-start.1
  122.8 1.1 copy.40
  123.9 4.0 %all-to-all-start = ((bf16[4,128,1024]{1,2,0:T(8,128)(2,1)}), bf16[4,128,1024]{1,2,0:T(8,128)(2,1)S(1)}, u32[]{:S(2)}, u32[]{:S(2)}) async-start(bf16[4,128,1024]{1,2,0:T(8,128)(2,1)} %copy.40), calls=%async_computation | async-start | bytes 2097152 | tf_op jit(solution)/shard_map/all_to_all | solution.py:62
  127.9 0.0 copy-done.1
  127.9 0.0 copy-start.3
  128.0 1.3 copy.41
  129.3 13.6 %all-to-all-done = bf16[4,128,1024]{1,2,0:T(8,128)(2,1)S(1)} async-done(((bf16[4,128,1024]{1,2,0:T(8,128)(2,1)}), bf16[4,128,1024]{1,2,0:T(8,128)(2,1)S(1)}, u32[]{:S(2)}, u32[]{:S(2)}) %all-to-all-start) | async-done | bytes 1048608 | tf_op jit(solution)/shard_map/all_to_all | solution.py:62
  142.8 3.5 %all-to-all-start.1 = ((bf16[4,128,1024]{1,2,0:T(8,128)(2,1)}), bf16[4,128,1024]{1,2,0:T(8,128)(2,1)S(1)}, u32[]{:S(2)}, u32[]{:S(2)}) async-start(bf16[4,128,1024]{1,2,0:T(8,128)(2,1)} %copy.41), calls=%async_computation.1 | async-start | bytes 2097152 | tf_op jit(solution)/shard_map/all_to_all | solution.py:63
  146.3 0.0 reduce-scatter.2.cloned.1.call-start
  146.4 0.0 copy-done.3
  146.4 0.6 fusion.5
  147.0 13.3 %all-to-all-done.1 = bf16[4,128,1024]{1,2,0:T(8,128)(2,1)S(1)} async-done(((bf16[4,128,1024]{1,2,0:T(8,128)(2,1)}), bf16[4,128,1024]{1,2,0:T(8,128)(2,1)S(1)}, u32[]{:S(2)}, u32[]{:S(2)}) %all-to-all-start.1) | async-done | bytes 1048608 | tf_op jit(solution)/shard_map/all_to_all | solution.py:63
  160.2 0.8 fusion.21
  161.0 15.2 %all_to_all.42 = bf16[128,4,1024]{0,2,1:T(8,128)(2,1)S(1)} all-to-all(bf16[128,4,1024]{0,2,1:T(8,128)(2,1)S(1)} %fusion.21), channel_id=1, replica_groups=mesh['seq'=64,'head'=4] {'head'}, dimensions={1} | all-to-all | bytes 2097152 | tf_op jit(solution)/shard_map/all_to_all | solution.py:69
  176.2 0.5 copy.42
  176.7 20.2 %all-gather.4.cloned.1.call-done = bf16[1024,4096]{0,1:T(8,128)(2,1)} async-done(((bf16[1024,64]{0,1:T(8,128)(2,1)}), bf16[1024,4096]{0,1:T(8,128)(2,1)}) %all-gather.4.cloned.1.call-update) | async-done | bytes 8388624 | tf_op jit(solution)/shard_map/all_gather | solution.py:72
  196.9 9.4 %convolution_convert_fusion = bf16[512,4096]{1,0:T(8,128)(2,1)} fusion(bf16[512,1024]{1,0:T(8,128)(2,1)S(1)} %bitcast.73, bf16[1024,4096]{0,1:T(8,128)(2,1)} %all-gather.4.cloned.1.call-done), kind=kOutput, calls=%fused_computation.2 | convolution fusion | flops 4297064448 | bytes 13631488 | tf_op jit(solution)/shard_map/dot_general | solution.py:70
  206.3 0.0 reduce-scatter.2.cloned.1.call-update
  206.4 94.8 %reduce-scatter.2.cloned.1.call-done = bf16[128,4096]{1,0:T(8,128)(2,1)} async-done(((bf16[512,4096]{1,0:T(8,128)(2,1)}), bf16[128,4096]{1,0:T(8,128)(2,1)}) %reduce-scatter.2.cloned.1.call-update) | async-done | bytes 1048592 | tf_op jit(solution)/shard_map/reduce_scatter | solution.py:75
  (3 shorter events, 0.1 us)
Async XLA Ops:
  6.5 108.7 %copy-start = (bf16[512,1024]{1,0:T(8,128)(2,1)S(1)}, bf16[512,1024]{1,0:T(8,128)(2,1)}, u32[]{:S(2)}) copy-start(bf16[512,1024]{1,0:T(8,128)(2,1)} %param.9) | copy-start | bytes 3145732
  6.5 107.5 %all-gather.6.cloned.1.call-start = ((), (), s32[]{:S(2)}) async-start(), calls=%async_computation.6 | async-start | bytes 17039360 | tf_op jit(solution)/shard_map/all_gather | solution.py:13
  9.4 187.4 %all-gather.4.cloned.1.call-start = ((), (), s32[]{:S(2)}) async-start(), calls=%async_computation.4 | async-start | bytes 8519680 | tf_op jit(solution)/shard_map/all_gather | solution.py:72
  114.1 1.2 copy-start.2
  122.8 5.1 %copy-start.1 = (bf16[512,1024]{1,0:T(8,128)(2,1)S(1)}, bf16[512,1024]{1,0:T(8,128)(2,1)}, u32[]{:S(2)}) copy-start(bf16[512,1024]{1,0:T(8,128)(2,1)} %param.12) | copy-start | bytes 3145732
  123.9 18.9 %all-to-all-start = ((bf16[4,128,1024]{1,2,0:T(8,128)(2,1)}), bf16[4,128,1024]{1,2,0:T(8,128)(2,1)S(1)}, u32[]{:S(2)}, u32[]{:S(2)}) async-start(bf16[4,128,1024]{1,2,0:T(8,128)(2,1)} %copy.40), calls=%async_computation | async-start | bytes 2097152 | tf_op jit(solution)/shard_map/all_to_all | solution.py:62
  127.9 18.4 %copy-start.3 = (f32[4096]{0:T(1024)S(1)}, f32[4096]{0:T(1024)}, u32[]{:S(2)}) copy-start(f32[4096]{0:T(1024)} %param.14) | copy-start | bytes 49156
  142.8 17.4 %all-to-all-start.1 = ((bf16[4,128,1024]{1,2,0:T(8,128)(2,1)}), bf16[4,128,1024]{1,2,0:T(8,128)(2,1)S(1)}, u32[]{:S(2)}, u32[]{:S(2)}) async-start(bf16[4,128,1024]{1,2,0:T(8,128)(2,1)} %copy.41), calls=%async_computation.1 | async-start | bytes 2097152 | tf_op jit(solution)/shard_map/all_to_all | solution.py:63
  146.3 154.8 %reduce-scatter.2.cloned.1.call-start = ((), (), s32[]{:S(2)}) async-start(), calls=%async_computation.5 | async-start | bytes 5242880 | tf_op jit(solution)/shard_map/reduce_scatter | solution.py:75
Sparse Core Ops, SparseCore 0:
  10.1 103.8 all-gather.5
  116.8 79.9 all-gather.3
  206.5 94.5 reduce-scatter.1
where the time goes:
time: 310 us; the launch traced here: 308 us
  waiting for transfers between devices  246 us (79%)
  matrix products  19.5 us (6%)
  blocking collectives  15.2 us (5%)
  between operations  13.2 us (4%)
  starting transfers between devices  7.63 us (2%)
  local copies, waits for them, and re-layouts  3.29 us (1%)
    all_gather x1, waiting for transfers between devices, entering(): gathered = lax.all_gather(value.astype(jnp.bfloat16), axis)  104 us
    reduce_scatter x1, waiting for transfers between devices, shards(): lax.psum_scatter(terms.astype(jnp.bfloat16), 'head', scatter_dimension=0,...  94.8 us
    all_gather x1, waiting for transfers between devices, shards(): lax.all_gather(out_weight, 'seq', axis=1, tiled=True)  20.2 us
    all_to_all x1, blocking collectives, shards(): lax.all_to_all(normed, 'head', split_axis=1, concat_axis=0, tiled=True)  15.2 us
    all_to_all x1, waiting for transfers between devices, shards(): lax.all_to_all(attn, 'head', split_axis=0, concat_axis=1, tiled=True)  13.6 us
    all_to_all x1, waiting for transfers between devices, shards(): lax.all_to_all(gate_input, 'head', split_axis=0, concat_axis=1, tiled=True)  13.3 us
    dot_general x1, matrix products, shards(): jnp.dot(hidden, lax.all_gather(out_weight, 'seq', axis=1, tiled=True), pr...  9.44 us
  transfers between devices with their start and end apart: 5, of which 5 were waited for; matrix products, arithmetic and copies ran while one was open for 4% of the time, Pallas kernels for 0%

commit v1 on v0

--- a/solution.py
+++ b/solution.py
@@ -69,7 +69,9 @@
     hidden = lax.all_to_all(normed, "head", split_axis=1, concat_axis=0, tiled=True)
     terms = jnp.dot(
         hidden,
-        lax.all_gather(out_weight, "seq", axis=1, tiled=True),
+        jnp.concatenate(
+            lax.all_to_all(jnp.stack([out_weight] * lax.axis_size("seq")), "seq", 0, 0), axis=1
+        ),
         preferred_element_type=jnp.float32,
     )
     return lax.psum_scatter(terms.astype(jnp.bfloat16), "head", scatter_dimension=0, tiled=True)

time: 310 us -> 506 us (1.63)
  waiting for transfers between devices: 246 us -> 361 us
  starting transfers between devices: 7.63 us -> 84 us
    all_to_all x0 -> x1, waiting for transfers between devices: none -> 185 us  [shards(): lax.all_to_all(jnp.stack([out_weight] * lax.axis_size('seq')), 'seq', 0, 0)]
    all_to_all x0 -> x1, starting transfers between devices: none -> 76.5 us  [shards(): lax.all_to_all(jnp.stack([out_weight] * lax.axis_size('seq')), 'seq', 0, 0)]
    reduce_scatter x1, waiting for transfers between devices: 94.8 us -> 44.3 us  [shards(): lax.psum_scatter(terms.astype(jnp.bfloat16), 'head', scatter_dimension=0,...]
    all_gather x1 -> x0, waiting for transfers between devices: 20.2 us -> none  [shards(): lax.all_gather(out_weight, 'seq', axis=1, tiled=True)]
  transfers between devices with their start and end apart: 5 -> 5, of which waited for: 5 -> 5; matrix products, arithmetic and copies ran while one was open for 4% -> 0% of each run, Pallas kernels for 0% -> 0%
where the time goes in v1:
time: 506 us; the launch traced here: 503 us
  waiting for transfers between devices  361 us (71%)
  starting transfers between devices  84 us (17%)
  matrix products  19.6 us (4%)
  blocking collectives  15.1 us (3%)
  between operations  13.5 us (3%)
  local copies, waits for them, and re-layouts  7.6 us (2%)
    all_to_all x1, waiting for transfers between devices, shards(): lax.all_to_all(jnp.stack([out_weight] * lax.axis_size('seq')), 'seq', 0, 0)  185 us
    all_gather x1, waiting for transfers between devices, entering(): gathered = lax.all_gather(value.astype(jnp.bfloat16), axis)  105 us
    all_to_all x1, starting transfers between devices, shards(): lax.all_to_all(jnp.stack([out_weight] * lax.axis_size('seq')), 'seq', 0, 0)  76.5 us
    reduce_scatter x1, waiting for transfers between devices, shards(): lax.psum_scatter(terms.astype(jnp.bfloat16), 'head', scatter_dimension=0,...  44.3 us
    all_to_all x1, blocking collectives, shards(): lax.all_to_all(normed, 'head', split_axis=1, concat_axis=0, tiled=True)  15.1 us
    all_to_all x1, waiting for transfers between devices, shards(): lax.all_to_all(attn, 'head', split_axis=0, concat_axis=1, tiled=True)  13.6 us
    all_to_all x1, waiting for transfers between devices, shards(): lax.all_to_all(gate_input, 'head', split_axis=0, concat_axis=1, tiled=True)  13.3 us
  transfers between devices with their start and end apart: 5, of which 5 were waited for; matrix products, arithmetic and copies ran while one was open for 0% of the time, Pallas kernels for 0%

profile of v1, /device:TPU:1, one launch (start us, length us, event | category | flops | bytes accessed | tf_op | source)
XLA Modules:
  0.0 503.3 jit_solution(13012139485158124862)
XLA Ops:
  6.5 0.0 copy-start
  6.5 0.0 all-gather.3.cloned.1.call-start
  6.5 2.9 fusion.34
  9.4 0.0 all-gather.3.cloned.1.call-update
  9.4 0.1 iota_compare_fusion
  9.5 104.5 %all-gather.3.cloned.1.call-done = bf16[512,128,128]{2,1,0:T(8,128)(2,1)} async-done(((bf16[8,128,128]{2,1,0:T(8,128)(2,1)}), bf16[512,128,128]{2,1,0:T(8,128)(2,1)}) %all-gather.3.cloned.1.call-update) | async-done | bytes 16777232 | tf_op jit(solution)/shard_map/all_gather | solution.py:13
  114.1 0.0 copy-start.2
  114.1 1.2 while.10
  114.1 1.1 convert_add_fusion.2
  115.3 0.0 copy-done
  115.3 0.0 copy-done.2
  115.3 2.4 fusion.13
  117.7 4.8 fusion.10
  122.5 0.3 all_to_all.35
  122.8 0.0 copy-start.1
  122.8 1.1 copy.41
  123.9 4.0 all-to-all-start
  127.9 0.0 copy-done.1
  127.9 0.0 copy-start.4
  128.0 1.3 copy.42
  129.3 13.6 %all-to-all-done = bf16[4,128,1024]{1,2,0:T(8,128)(2,1)S(1)} async-done(((bf16[4,128,1024]{1,2,0:T(8,128)(2,1)}), bf16[4,128,1024]{1,2,0:T(8,128)(2,1)S(1)}, u32[]{:S(2)}, u32[]{:S(2)}) %all-to-all-start) | async-done | bytes 1048608 | tf_op jit(solution)/shard_map/all_to_all | solution.py:62
  142.8 3.5 all-to-all-start.1
  146.3 0.0 copy-done.4
  146.4 0.6 fusion.5
  146.9 0.0 copy-start.3
  146.9 13.3 %all-to-all-done.1 = bf16[4,128,1024]{1,2,0:T(8,128)(2,1)S(1)} async-done(((bf16[4,128,1024]{1,2,0:T(8,128)(2,1)}), bf16[4,128,1024]{1,2,0:T(8,128)(2,1)S(1)}, u32[]{:S(2)}, u32[]{:S(2)}) %all-to-all-start.1) | async-done | bytes 1048608 | tf_op jit(solution)/shard_map/all_to_all | solution.py:63
  160.2 0.8 fusion.21
  161.0 15.1 %all_to_all.47 = bf16[128,4,1024]{0,2,1:T(8,128)(2,1)S(1)} all-to-all(bf16[128,4,1024]{0,2,1:T(8,128)(2,1)S(1)} %fusion.21), channel_id=1, replica_groups=mesh['seq'=64,'head'=4] {'head'}, dimensions={1} | all-to-all | bytes 2097152 | tf_op jit(solution)/shard_map/all_to_all | solution.py:69
  176.1 0.0 copy-done.3
  176.2 4.3 stack.2
  180.5 76.5 %all-to-all-start.3 = ((bf16[64,1024,64]{1,2,0:T(8,128)(2,1)}), bf16[64,1024,64]{1,2,0:T(8,128)(2,1)}, u32[]{:S(2)}, u32[]{:S(2)}) async-start(bf16[64,1024,64]{1,2,0:T(8,128)(2,1)} %stack.2), calls=%async_computation.3 | async-start | bytes 16777216 | tf_op jit(solution)/shard_map/all_to_all | solution.py:73
  256.9 0.0 reduce-scatter.2.cloned.1.call-start
  257.0 0.5 copy.43
  257.5 185.2 %all-to-all-done.3 = bf16[64,1024,64]{1,2,0:T(8,128)(2,1)} async-done(((bf16[64,1024,64]{1,2,0:T(8,128)(2,1)}), bf16[64,1024,64]{1,2,0:T(8,128)(2,1)}, u32[]{:S(2)}, u32[]{:S(2)}) %all-to-all-start.3) | async-done | bytes 8388640 | tf_op jit(solution)/shard_map/all_to_all | solution.py:73
  442.7 9.5 %convolution_convert_fusion = bf16[512,4096]{1,0:T(8,128)(2,1)} fusion(bf16[512,1024]{1,0:T(8,128)(2,1)S(1)} %bitcast.76, bf16[1024,4096]{0,1:T(8,128)(2,1)} %bitcast.10), kind=kOutput, calls=%fused_computation.2 | convolution fusion | flops 4297064448 | bytes 13631488 | tf_op jit(solution)/shard_map/dot_general | solution.py:70
  452.1 0.0 reduce-scatter.2.cloned.1.call-update
  452.2 44.3 %reduce-scatter.2.cloned.1.call-done = bf16[128,4096]{1,0:T(8,128)(2,1)} async-done(((bf16[512,4096]{1,0:T(8,128)(2,1)}), bf16[128,4096]{1,0:T(8,128)(2,1)}) %reduce-scatter.2.cloned.1.call-update) | async-done | bytes 1048592 | tf_op jit(solution)/shard_map/reduce_scatter | solution.py:77
  (3 shorter events, 0.1 us)
Async XLA Ops:
  6.5 108.7 %copy-start = (bf16[512,1024]{1,0:T(8,128)(2,1)S(1)}, bf16[512,1024]{1,0:T(8,128)(2,1)}, u32[]{:S(2)}) copy-start(bf16[512,1024]{1,0:T(8,128)(2,1)} %param.9) | copy-start | bytes 3145732
  6.5 107.5 %all-gather.3.cloned.1.call-start = ((), (), s32[]{:S(2)}) async-start(), calls=%async_computation.6 | async-start | bytes 17039360 | tf_op jit(solution)/shard_map/all_gather | solution.py:13
  114.1 1.2 copy-start.2
  122.8 5.1 %copy-start.1 = (bf16[512,1024]{1,0:T(8,128)(2,1)S(1)}, bf16[512,1024]{1,0:T(8,128)(2,1)}, u32[]{:S(2)}) copy-start(bf16[512,1024]{1,0:T(8,128)(2,1)} %param.12) | copy-start | bytes 3145732
  123.9 18.9 %all-to-all-start = ((bf16[4,128,1024]{1,2,0:T(8,128)(2,1)}), bf16[4,128,1024]{1,2,0:T(8,128)(2,1)S(1)}, u32[]{:S(2)}, u32[]{:S(2)}) async-start(bf16[4,128,1024]{1,2,0:T(8,128)(2,1)} %copy.41), calls=%async_computation | async-start | bytes 2097152 | tf_op jit(solution)/shard_map/all_to_all | solution.py:62
  127.9 18.4 %copy-start.4 = (f32[4096]{0:T(1024)S(1)}, f32[4096]{0:T(1024)}, u32[]{:S(2)}) copy-start(f32[4096]{0:T(1024)} %param.14) | copy-start | bytes 49156
  142.8 17.4 %all-to-all-start.1 = ((bf16[4,128,1024]{1,2,0:T(8,128)(2,1)}), bf16[4,128,1024]{1,2,0:T(8,128)(2,1)S(1)}, u32[]{:S(2)}, u32[]{:S(2)}) async-start(bf16[4,128,1024]{1,2,0:T(8,128)(2,1)} %copy.42), calls=%async_computation.1 | async-start | bytes 2097152 | tf_op jit(solution)/shard_map/all_to_all | solution.py:63
  146.9 29.2 %copy-start.3 = (bf16[1024,64]{0,1:T(8,128)(2,1)S(1)}, bf16[1024,64]{0,1:T(8,128)(2,1)}, u32[]{:S(2)}) copy-start(bf16[1024,64]{0,1:T(8,128)(2,1)} %param.15) | copy-start | bytes 393220
  180.5 262.2 %all-to-all-start.3 = ((bf16[64,1024,64]{1,2,0:T(8,128)(2,1)}), bf16[64,1024,64]{1,2,0:T(8,128)(2,1)}, u32[]{:S(2)}, u32[]{:S(2)}) async-start(bf16[64,1024,64]{1,2,0:T(8,128)(2,1)} %stack.2), calls=%async_computation.3 | async-start | bytes 16777216 | tf_op jit(solution)/shard_map/all_to_all | solution.py:73
  256.9 239.5 %reduce-scatter.2.cloned.1.call-start = ((), (), s32[]{:S(2)}) async-start(), calls=%async_computation.5 | async-start | bytes 5242880 | tf_op jit(solution)/shard_map/reduce_scatter | solution.py:77
Sparse Core Ops, SparseCore 0:
  10.1 103.8 all-gather.2
  452.3 44.1 reduce-scatter.1
